TPU v7x, 512 devices: a whole 4x4x16 slice. The times are simulated.
512 devices in a mesh: dp: 16 (over y, z_lo), ctx: 32 (over x, z_hi, core).
Axes of the slice: x: 4, y: 4, z: 16 (z_hi: 4, z_lo: 4; z = z_hi * 4 + z_lo), core: 2. Of those that a mesh axis runs over, the one named last changes fastest.
Arguments:
- queries: bfloat16 [16, 4096, 512], P('dp', 'ctx'), may hold values from -6 to 6
- keys: bfloat16 [16, 4096, 512], P('dp', 'ctx'), may hold values from -6 to 6
- values: bfloat16 [16, 4096, 512], P('dp', 'ctx'), may hold values from -6 to 6
- grad_out: bfloat16 [16, 4096, 512], P('dp', 'ctx'), may hold values from -6 to 6
- filter_taps: float32 [4096, 512], P('ctx'), may hold values from -0.125 to 0.125
Outputs:
- conv_out: bfloat16 [16, 4096, 512], P('dp', 'ctx')
- grad_queries: bfloat16 [16, 4096, 512], P('dp', 'ctx')
- grad_keys: bfloat16 [16, 4096, 512], P('dp', 'ctx')
- grad_values: bfloat16 [16, 4096, 512], P('dp', 'ctx')
- grad_filter: float32 [4096, 512], P('ctx')
All inputs are finite; a program needn't handle non-finite values.
Results may differ from a plain program's by a relative error of at most 0.0023.
Values sent between devices are 32-bit elements; how exact they have to be, the bound alone decides.
No kernel may reach another device: no remote copies, remote signals or barrier semaphores. Data moves between devices by JAX's collectives and lax.ppermute only.
A program may use at most 64 MiB of HBM per device.

v0:
```python
import math
import jax
import jax.numpy as jnp
from jax import lax
from jax.sharding import PartitionSpec as P


def angle_table(numer, denom):
    angle = 2.0 * math.pi / denom * (numer % denom).astype(jnp.float32)
    return (jnp.cos(angle), jnp.sin(angle))


def exact_dot(left, right):
    return jnp.dot(left, right, precision=lax.Precision.HIGHEST)


def exact_mix(table, operand):
    return jnp.einsum("kb,abc->akc", table, operand, precision=lax.Precision.HIGHEST)


def owned_harmonics(blocks):
    rows = lax.iota(jnp.int32, 2 * blocks)
    half_row = rows // 2
    mirrored = jnp.where(half_row == 0, blocks, 2 * blocks - half_row)
    return jnp.where(rows % 2 == 0, half_row, mirrored)


def forward_spectrum(real_in):
    blocks = lax.axis_size("ctx")
    tokens, width = real_in.shape
    stride = tokens // blocks
    period = 2 * blocks * tokens
    total_width = real_in.shape[1]
    columns = lax.all_to_all(
        real_in.reshape(1, tokens, total_width), "ctx", split_axis=1, concat_axis=0, tiled=True
    )
    harmonic = owned_harmonics(blocks)
    source = lax.iota(jnp.int32, blocks)
    cos_mix, sin_mix = angle_table(harmonic[:, None] * source[None, :], 2 * blocks)
    flat_real = columns.reshape(blocks, stride * width)
    real_part = exact_dot(cos_mix, flat_real)
    imag_part = -exact_dot(sin_mix, flat_real)
    real_part = real_part.reshape(2 * blocks, stride, width)
    imag_part = imag_part.reshape(2 * blocks, stride, width)
    offsets = lax.axis_index("ctx") * stride + lax.iota(jnp.int32, stride)
    cos_turn, sin_turn = angle_table(harmonic[:, None] * offsets[None, :], period)
    cos_turn = cos_turn[:, :, None]
    sin_turn = sin_turn[:, :, None]
    rotated = jnp.stack(
        [real_part * cos_turn + imag_part * sin_turn, imag_part * cos_turn - real_part * sin_turn]
    )
    spectral = lax.all_to_all(rotated, "ctx", split_axis=1, concat_axis=2, tiled=True)
    position = lax.iota(jnp.int32, tokens)
    cos_full, sin_full = angle_table(position[:, None] * position[None, :], tokens)
    out_real = exact_mix(cos_full, spectral[0]) + exact_mix(sin_full, spectral[1])
    out_imag = exact_mix(cos_full, spectral[1]) - exact_mix(sin_full, spectral[0])
    return (out_real, out_imag)


def transform_pairs(first, second):
    width = first.shape[1]
    all_real, all_imag = forward_spectrum(jnp.concatenate([first, second], 1))
    return (
        all_real[..., :width],
        all_imag[..., :width],
        all_real[..., width:],
        all_imag[..., width:],
    )


def inverse_tokens(spec_real, spec_imag):
    blocks = lax.axis_size("ctx")
    tokens = spec_real.shape[1]
    channels = spec_real.shape[2]
    stride = tokens // blocks
    period = 2 * blocks * tokens
    position = lax.iota(jnp.int32, tokens)
    cos_full, sin_full = angle_table(position[:, None] * position[None, :], tokens)
    back_real = exact_mix(cos_full, spec_real) - exact_mix(sin_full, spec_imag)
    back_imag = exact_mix(sin_full, spec_real) + exact_mix(cos_full, spec_imag)
    harmonic = owned_harmonics(blocks)
    local_freq = lax.dynamic_slice_in_dim(harmonic, 2 * lax.axis_index("ctx"), 2)
    cos_turn, sin_turn = angle_table(local_freq[:, None] * position[None, :], period)
    cos_turn = cos_turn[:, :, None]
    sin_turn = sin_turn[:, :, None]
    rotated = jnp.stack(
        [back_real * cos_turn - back_imag * sin_turn, back_real * sin_turn + back_imag * cos_turn]
    )
    gathered = lax.all_to_all(rotated, "ctx", split_axis=2, concat_axis=1, tiled=True)
    source = lax.iota(jnp.int32, blocks)
    cos_mix, sin_mix = angle_table(source[:, None] * harmonic[None, :], 2 * blocks)
    flat_real = gathered[0].reshape(2 * blocks, stride * channels)
    flat_imag = gathered[1].reshape(2 * blocks, stride * channels)
    finished = (exact_dot(cos_mix, flat_real) - exact_dot(sin_mix, flat_imag)) * (1.0 / period)
    finished = finished.reshape(blocks, stride, channels)
    returned = lax.all_to_all(finished, "ctx", split_axis=0, concat_axis=1, tiled=True)
    return returned.reshape(tokens, finished.shape[2])


def inverse_pairs(first_real, first_imag, second_real, second_imag):
    width = first_real.shape[2]
    timed = inverse_tokens(
        jnp.concatenate([first_real, second_real], 2), jnp.concatenate([first_imag, second_imag], 2)
    )
    return (timed[:, :width], timed[:, width:])


def local(queries, keys, values, grad_out, filter_taps):
    query_f = queries[0].astype(jnp.float32)
    key_f = keys[0].astype(jnp.float32)
    value_f = values[0].astype(jnp.float32)
    grad_f = grad_out[0].astype(jnp.float32)
    gated = key_f * value_f
    grad_s = grad_f * query_f
    channels = query_f.shape[1]
    half_width = channels // 2
    groups = lax.axis_size("dp")
    per_group = channels // groups
    half_group = per_group // 2
    gated_real, gated_imag, grad_real, grad_imag = transform_pairs(gated, grad_s)
    filter_part = lax.dynamic_slice_in_dim(
        filter_taps, lax.axis_index("dp") * per_group, per_group, 1
    )
    low_real, low_imag, high_real, high_imag = transform_pairs(
        filter_part[:, :half_group], filter_part[:, half_group:]
    )
    own_real = jnp.concatenate([low_real, high_real], 2)
    own_imag = jnp.concatenate([low_imag, high_imag], 2)
    taps_real, taps_imag = (
        lax.all_gather(own_real, "dp", axis=2, tiled=True),
        lax.all_gather(own_imag, "dp", axis=2, tiled=True),
    )
    conv_real = taps_real * gated_real - taps_imag * gated_imag
    conv_imag = taps_real * gated_imag + taps_imag * gated_real
    back_real = taps_real * grad_real + taps_imag * grad_imag
    back_imag = taps_real * grad_imag - taps_imag * grad_real
    lag_real = grad_real * gated_real + grad_imag * gated_imag
    lag_imag = grad_imag * gated_real - grad_real * gated_imag
    grad_scale = 1.0 / math.sqrt(groups * lax.axis_size("ctx") * query_f.shape[0])
    first_time, second_time = inverse_pairs(
        jnp.concatenate([conv_real, lag_real[..., :half_width]], 2),
        jnp.concatenate([conv_imag, lag_imag[..., :half_width]], 2),
        jnp.concatenate([back_real, lag_real[..., half_width:]], 2),
        jnp.concatenate([back_imag, lag_imag[..., half_width:]], 2),
    )
    conv_s = first_time[:, :channels]
    grad_z = second_time[:, :channels]
    lag_grad = jnp.concatenate([first_time[:, channels:], second_time[:, channels:]], 1)
    grad_filter = lax.psum(lag_grad, "dp") * grad_scale
    conv_out = (query_f * conv_s).astype(jnp.bfloat16)[None]
    grad_queries = (grad_f * conv_s).astype(jnp.bfloat16)[None]
    grad_keys = (grad_z * value_f).astype(jnp.bfloat16)[None]
    grad_values = (grad_z * key_f).astype(jnp.bfloat16)[None]
    return (conv_out, grad_queries, grad_keys, grad_values, grad_filter)


def solution(mesh):
    return jax.shard_map(
        local,
        mesh=mesh,
        in_specs=(
            P("dp", "ctx", None),
            P("dp", "ctx", None),
            P("dp", "ctx", None),
            P("dp", "ctx", None),
            P("ctx", None),
        ),
        out_specs=(
            P("dp", "ctx", None),
            P("dp", "ctx", None),
            P("dp", "ctx", None),
            P("dp", "ctx", None),
            P("ctx", None),
        ),
        check_vma=False,
    )
```

profile of v0, /device:TPU:2, one launch (start us, length us, event | category | flops | bytes accessed | tf_op | source)
XLA Modules:
  0.0 685.8 jit_solution(10451977138814739588)
XLA Ops:
  10.2 18.2 %all-to-all-start = ((f32[32,1,128]{2,1,0:T(1,128)}), f32[32,1,128]{2,1,0:T(1,128)S(1)}, u32[]{:S(2)}, u32[]{:S(2)}) async-start(f32[32,1,128]{2,1,0:T(1,128)} %reshape.270), calls=%async_computation | async-start | bytes 32768 | tf_op jit(solution)/shard_map/all_to_all | solution.py:34
  28.5 1.2 convert_multiply_fusion.1
  29.7 1.2 reshape.248
  30.9 10.9 %all-to-all-done = f32[32,1,128]{2,1,0:T(1,128)S(1)} async-done(((f32[32,1,128]{2,1,0:T(1,128)}), f32[32,1,128]{2,1,0:T(1,128)S(1)}, u32[]{:S(2)}, u32[]{:S(2)}) %all-to-all-start) | async-done | bytes 16416 | tf_op jit(solution)/shard_map/all_to_all | solution.py:34
  41.8 5.0 all-to-all-start.2
  51.0 22.9 %all-to-all-done.2 = f32[1,128,1024]{2,0,1:T(1,128)S(1)} async-done(((f32[1,128,1024]{2,0,1:T(1,128)}), f32[1,128,1024]{2,0,1:T(1,128)S(1)}, u32[]{:S(2)}, u32[]{:S(2)}) %all-to-all-start.2) | async-done | bytes 524320 | tf_op jit(solution)/shard_map/all_to_all | solution.py:34
  74.0 9.7 %all-to-all-start.1 = ((f32[32,1,512]{2,1,0:T(1,128)}), f32[32,1,512]{2,1,0:T(1,128)S(1)}, u32[]{:S(2)}, u32[]{:S(2)}) async-start(f32[32,1,512]{2,1,0:T(1,128)} %reshape.272), calls=%async_computation.1 | async-start | bytes 131072 | tf_op jit(solution)/shard_map/all_to_all | solution.py:52
  83.7 1.2 reduce.1
  85.2 1.1 convolution_negate_fusion
  86.3 1.3 fusion.6
  87.9 2.7 copy.46
  90.6 6.8 all-to-all-done.1
  97.4 7.8 %all-to-all-start.3 = ((f32[2,64,4,1024]{3,2,0,1:T(4,128)}), f32[2,64,4,1024]{3,2,0,1:T(4,128)S(1)}, u32[]{:S(2)}, u32[]{:S(2)}) async-start(f32[2,64,4,1024]{3,2,0,1:T(4,128)} %copy.46), calls=%async_computation.3 | async-start | bytes 4194304 | tf_op jit(solution)/shard_map/all_to_all | solution.py:52
  108.6 130.4 %all_gather.7 = f32[2,128,512]{1,2,0:T(8,128)} all-gather(f32[2,128,32]{1,2,0:T(8,128)S(1)} %fusion.3), channel_id=1, replica_groups=mesh['dp'=16,'ctx'=32] {'dp'}, dimensions={2}, use_global_device_ids=true | all-gather | bytes 557056 | tf_op jit(solution)/shard_map/all_gather | solution.py:131
  239.0 44.2 %all_gather.6 = f32[2,128,512]{1,2,0:T(8,128)} all-gather(f32[2,128,32]{1,2,0:T(8,128)S(1)} %fusion.4), channel_id=1, replica_groups=mesh['dp'=16,'ctx'=32] {'dp'}, dimensions={2}, use_global_device_ids=true | all-gather | bytes 557056 | tf_op jit(solution)/shard_map/all_gather | solution.py:130
  283.3 1.9 copy.75
  285.2 1.3 fusion.171
  287.5 1.2 fusion.33
  288.8 1.2 fusion.37
  290.0 1.2 fusion.1
  291.3 1.3 fusion.2
  293.0 1.7 fusion.9
  294.7 1.6 fusion.10
  296.4 1.7 convolution_add_fusion
  298.1 2.2 subtract_bitcast_fusion
  300.5 3.6 copy.54
  304.1 153.5 %all_to_all.72 = f32[2,2,128,1536]{3,1,0,2:T(2,128)S(1)} all-to-all(f32[2,2,128,1536]{3,1,0,2:T(2,128)} %copy.54), channel_id=1, replica_groups=mesh['dp'=16,'ctx'=32] {'ctx'}, dimensions={2} | all-to-all | bytes 6291456 | tf_op jit(solution)/shard_map/all_to_all | solution.py:89
  457.5 1.1 copy.55
  458.6 1.1 fusion.170
  463.9 50.3 %all_to_all.73 = f32[32,4,1536]{2,1,0:T(4,128)S(1)} all-to-all(f32[32,4,1536]{2,1,0:T(4,128)S(1)} %reshape.251), channel_id=1, replica_groups=mesh['dp'=16,'ctx'=32] {'ctx'}, dimensions={0} | all-to-all | bytes 1572864 | tf_op jit(solution)/shard_map/all_to_all | solution.py:96
  516.2 161.1 %all-reduce.2.cloned.1.call-done = f32[128,512]{1,0:T(8,128)} async-done(((f32[128,512]{1,0:T(8,128)}), f32[128,512]{1,0:T(8,128)}) %all-reduce.2.cloned.1.call-update) | async-done | bytes 262160 | tf_op jit(solution)/shard_map/psum | solution.py:149
  677.3 1.7 broadcast_multiply_fusion
  (68 shorter events, 18.8 us)
Async XLA Ops:
  7.2 1.0 copy-start
  10.2 31.6 %all-to-all-start = ((f32[32,1,128]{2,1,0:T(1,128)}), f32[32,1,128]{2,1,0:T(1,128)S(1)}, u32[]{:S(2)}, u32[]{:S(2)}) async-start(f32[32,1,128]{2,1,0:T(1,128)} %reshape.270), calls=%async_computation | async-start | bytes 32768 | tf_op jit(solution)/shard_map/all_to_all | solution.py:34
  41.8 32.2 %all-to-all-start.2 = ((f32[1,128,1024]{2,0,1:T(1,128)}), f32[1,128,1024]{2,0,1:T(1,128)S(1)}, u32[]{:S(2)}, u32[]{:S(2)}) async-start(f32[1,128,1024]{2,0,1:T(1,128)} %reshape.248), calls=%async_computation.2 | async-start | bytes 1048576 | tf_op jit(solution)/shard_map/all_to_all | solution.py:34
  74.0 23.4 %all-to-all-start.1 = ((f32[32,1,512]{2,1,0:T(1,128)}), f32[32,1,512]{2,1,0:T(1,128)S(1)}, u32[]{:S(2)}, u32[]{:S(2)}) async-start(f32[32,1,512]{2,1,0:T(1,128)} %reshape.272), calls=%async_computation.1 | async-start | bytes 131072 | tf_op jit(solution)/shard_map/all_to_all | solution.py:52
  97.4 185.9 %all-to-all-start.3 = ((f32[2,64,4,1024]{3,2,0,1:T(4,128)}), f32[2,64,4,1024]{3,2,0,1:T(4,128)S(1)}, u32[]{:S(2)}, u32[]{:S(2)}) async-start(f32[2,64,4,1024]{3,2,0,1:T(4,128)} %copy.46), calls=%async_computation.3 | async-start | bytes 4194304 | tf_op jit(solution)/shard_map/all_to_all | solution.py:52
  105.2 572.1 %all-reduce.2.cloned.1.call-start = ((), (), s32[]{:S(2)}) async-start(), calls=%async_computation.6 | async-start | bytes 524288 | tf_op jit(solution)/shard_map/psum | solution.py:149
  291.2 1.3 copy-start.1
  291.3 1.3 copy-start.2
  514.2 1.1 copy-start.3
  514.2 1.1 copy-start.4
  514.2 1.1 copy-start.5
  514.3 1.1 copy-start.6
Sparse Core Ops, SparseCore 0:
  515.4 161.7 all-reduce.1
where the time goes:
time: 686 us
  blocking collectives  378 us (55%)
  waiting for transfers between devices  202 us (29%)
  starting transfers between devices  40.8 us (6%)
  local copies, waits for them, and re-layouts  22.2 us (3%)
  matrix products  19 us (3%)
  between operations  14.6 us (2%)
  other arithmetic  9.08 us (1%)
    psum x1, waiting for transfers between devices, local(): grad_filter = lax.psum(lag_grad, 'dp') * grad_scale  161 us
    all_to_all x1, blocking collectives, inverse_tokens(): lax.all_to_all(rotated, 'ctx', split_axis=2, concat_axis=1, tiled=True)  153 us
    all_gather x1, blocking collectives, local(): lax.all_gather(own_imag, 'dp', axis=2, tiled=True)  130 us
    all_to_all x1, blocking collectives, inverse_tokens(): lax.all_to_all(finished, 'ctx', split_axis=0, concat_axis=1, tiled=True)  50.3 us
    all_gather x1, blocking collectives, local(): lax.all_gather(own_real, 'dp', axis=2, tiled=True)  44.2 us
    all_to_all x2, waiting for transfers between devices, forward_spectrum(): lax.all_to_all(real_in.reshape(1, tokens, total_width), 'ctx', split_axis...  33.9 us
    all_to_all x2, starting transfers between devices, forward_spectrum(): lax.all_to_all(real_in.reshape(1, tokens, total_width), 'ctx', split_axis...  23.2 us
    all_to_all x2, starting transfers between devices, forward_spectrum(): lax.all_to_all(rotated, 'ctx', split_axis=1, concat_axis=2, tiled=True)  17.5 us
  transfers between devices with their start and end apart: 5, of which 4 were waited for; matrix products, arithmetic and copies ran while one was open for 3% of the time, Pallas kernels for 0%

commit v1 on v0

--- a/solution.py
+++ b/solution.py
@@ -146,7 +146,7 @@
     conv_s = first_time[:, :channels]
     grad_z = second_time[:, :channels]
     lag_grad = jnp.concatenate([first_time[:, channels:], second_time[:, channels:]], 1)
-    grad_filter = lax.psum(lag_grad, "dp") * grad_scale
+    grad_filter = jnp.sum(lax.all_gather(lag_grad, "dp"), axis=0) * grad_scale
     conv_out = (query_f * conv_s).astype(jnp.bfloat16)[None]
     grad_queries = (grad_f * conv_s).astype(jnp.bfloat16)[None]
     grad_keys = (grad_z * value_f).astype(jnp.bfloat16)[None]

time: 686 us -> 645 us (0.940)
  the two profiles are of different devices: /device:TPU:2 before, /device:TPU:1 now
where the time goes in v1:
time: 645 us; the launch traced here: 636 us
  blocking collectives  390 us (60%)
  waiting for transfers between devices  142 us (22%)
  starting transfers between devices  37.2 us (6%)
  local copies, waits for them, and re-layouts  22.2 us (3%)
  matrix products  18.9 us (3%)
  between operations  15 us (2%)
  other arithmetic  10.8 us (2%)
    all_to_all x1, blocking collectives, inverse_tokens(): lax.all_to_all(rotated, 'ctx', split_axis=2, concat_axis=1, tiled=True)  170 us
    all_gather x1, blocking collectives, local(): lax.all_gather(own_imag, 'dp', axis=2, tiled=True)  125 us
    all_gather x1, waiting for transfers between devices, local(): grad_filter = jnp.sum(lax.all_gather(lag_grad, 'dp'), axis=0) * grad_scale  96.9 us
    all_gather x1, blocking collectives, local(): lax.all_gather(own_real, 'dp', axis=2, tiled=True)  47.8 us
    all_to_all x1, blocking collectives, inverse_tokens(): lax.all_to_all(finished, 'ctx', split_axis=0, concat_axis=1, tiled=True)  47.7 us
    all_to_all x2, waiting for transfers between devices, forward_spectrum(): lax.all_to_all(real_in.reshape(1, tokens, total_width), 'ctx', split_axis...  36.2 us
    all_to_all x2, starting transfers between devices, forward_spectrum(): lax.all_to_all(real_in.reshape(1, tokens, total_width), 'ctx', split_axis...  23.4 us
    dot_general x12, matrix products, exact_mix(): jnp.einsum('kb,abc->akc', table, operand, precision=lax.Precision.HIGHEST)  14.1 us
  transfers between devices with their start and end apart: 5, of which 4 were waited for; matrix products, arithmetic and copies ran while one was open for 3% of the time, Pallas kernels for 0%

profile of v1, /device:TPU:1, one launch (start us, length us, event | category | flops | bytes accessed | tf_op | source)
XLA Modules:
  0.0 636.3 jit_solution(11207311116779306053)
XLA Ops:
  10.2 19.2 %all-to-all-start = ((f32[32,1,128]{2,1,0:T(1,128)}), f32[32,1,128]{2,1,0:T(1,128)S(1)}, u32[]{:S(2)}, u32[]{:S(2)}) async-start(f32[32,1,128]{2,1,0:T(1,128)} %reshape.271), calls=%async_computation | async-start | bytes 32768 | tf_op jit(solution)/shard_map/all_to_all | solution.py:34
  29.5 1.2 convert_multiply_fusion.1
  30.7 1.1 reshape.248
  31.8 11.7 %all-to-all-done = f32[32,1,128]{2,1,0:T(1,128)S(1)} async-done(((f32[32,1,128]{2,1,0:T(1,128)}), f32[32,1,128]{2,1,0:T(1,128)S(1)}, u32[]{:S(2)}, u32[]{:S(2)}) %all-to-all-start) | async-done | bytes 16416 | tf_op jit(solution)/shard_map/all_to_all | solution.py:34
  43.6 4.2 all-to-all-start.2
  52.0 24.5 %all-to-all-done.2 = f32[1,128,1024]{2,0,1:T(1,128)S(1)} async-done(((f32[1,128,1024]{2,0,1:T(1,128)}), f32[1,128,1024]{2,0,1:T(1,128)S(1)}, u32[]{:S(2)}, u32[]{:S(2)}) %all-to-all-start.2) | async-done | bytes 524320 | tf_op jit(solution)/shard_map/all_to_all | solution.py:34
  76.4 8.2 %all-to-all-start.1 = ((f32[32,1,512]{2,1,0:T(1,128)}), f32[32,1,512]{2,1,0:T(1,128)S(1)}, u32[]{:S(2)}, u32[]{:S(2)}) async-start(f32[32,1,512]{2,1,0:T(1,128)} %reshape.273), calls=%async_computation.1 | async-start | bytes 131072 | tf_op jit(solution)/shard_map/all_to_all | solution.py:52
  84.7 1.2 reduce.1
  86.2 1.1 convolution_negate_fusion
  87.3 1.3 fusion.6
  88.8 2.7 copy.46
  91.5 9.1 %all-to-all-done.1 = f32[32,1,512]{2,1,0:T(1,128)S(1)} async-done(((f32[32,1,512]{2,1,0:T(1,128)}), f32[32,1,512]{2,1,0:T(1,128)S(1)}, u32[]{:S(2)}, u32[]{:S(2)}) %all-to-all-start.1) | async-done | bytes 65568 | tf_op jit(solution)/shard_map/all_to_all | solution.py:52
  100.6 5.5 all-to-all-start.3
  109.6 124.5 %all_gather.13 = f32[2,128,512]{1,2,0:T(8,128)} all-gather(f32[2,128,32]{1,2,0:T(8,128)S(1)} %fusion.3), channel_id=1, replica_groups=mesh['dp'=16,'ctx'=32] {'dp'}, dimensions={2}, use_global_device_ids=true | all-gather | bytes 557056 | tf_op jit(solution)/shard_map/all_gather | solution.py:131
  234.1 47.8 %all_gather.12 = f32[2,128,512]{1,2,0:T(8,128)} all-gather(f32[2,128,32]{1,2,0:T(8,128)S(1)} %fusion.4), channel_id=1, replica_groups=mesh['dp'=16,'ctx'=32] {'dp'}, dimensions={2}, use_global_device_ids=true | all-gather | bytes 557056 | tf_op jit(solution)/shard_map/all_gather | solution.py:130
  282.0 1.9 copy.75
  283.9 1.3 fusion.171
  286.2 1.2 fusion.33
  287.5 1.2 fusion.37
  288.7 1.2 fusion.1
  290.0 1.3 fusion.2
  291.7 1.7 fusion.9
  293.4 1.7 fusion.10
  295.1 1.7 convolution_add_fusion
  296.9 2.1 subtract_bitcast_fusion
  299.2 3.6 copy.54
  302.8 169.9 %all_to_all.72 = f32[2,2,128,1536]{3,1,0,2:T(2,128)S(1)} all-to-all(f32[2,2,128,1536]{3,1,0,2:T(2,128)} %copy.54), channel_id=1, replica_groups=mesh['dp'=16,'ctx'=32] {'ctx'}, dimensions={2} | all-to-all | bytes 6291456 | tf_op jit(solution)/shard_map/all_to_all | solution.py:89
  472.7 1.1 copy.55
  473.8 1.1 fusion.170
  479.1 47.7 %all_to_all.73 = f32[32,4,1536]{2,1,0:T(4,128)S(1)} all-to-all(f32[32,4,1536]{2,1,0:T(4,128)S(1)} %reshape.251), channel_id=1, replica_groups=mesh['dp'=16,'ctx'=32] {'ctx'}, dimensions={0} | all-to-all | bytes 1572864 | tf_op jit(solution)/shard_map/all_to_all | solution.py:96
  528.7 96.9 %all-gather.3.cloned.1.call-done = f32[2048,512]{1,0:T(8,128)} async-done(((f32[128,512]{1,0:T(8,128)}), f32[2048,512]{1,0:T(8,128)}) %all-gather.3.cloned.1.call-update) | async-done | bytes 4194320 | tf_op jit(solution)/shard_map/all_gather | solution.py:149
  625.7 2.7 reduce_sum.9
  (71 shorter events, 19.6 us)
Async XLA Ops:
  7.2 1.0 copy-start
  10.2 33.3 %all-to-all-start = ((f32[32,1,128]{2,1,0:T(1,128)}), f32[32,1,128]{2,1,0:T(1,128)S(1)}, u32[]{:S(2)}, u32[]{:S(2)}) async-start(f32[32,1,128]{2,1,0:T(1,128)} %reshape.271), calls=%async_computation | async-start | bytes 32768 | tf_op jit(solution)/shard_map/all_to_all | solution.py:34
  43.6 32.9 %all-to-all-start.2 = ((f32[1,128,1024]{2,0,1:T(1,128)}), f32[1,128,1024]{2,0,1:T(1,128)S(1)}, u32[]{:S(2)}, u32[]{:S(2)}) async-start(f32[1,128,1024]{2,0,1:T(1,128)} %reshape.248), calls=%async_computation.2 | async-start | bytes 1048576 | tf_op jit(solution)/shard_map/all_to_all | solution.py:34
  76.4 24.1 %all-to-all-start.1 = ((f32[32,1,512]{2,1,0:T(1,128)}), f32[32,1,512]{2,1,0:T(1,128)S(1)}, u32[]{:S(2)}, u32[]{:S(2)}) async-start(f32[32,1,512]{2,1,0:T(1,128)} %reshape.273), calls=%async_computation.1 | async-start | bytes 131072 | tf_op jit(solution)/shard_map/all_to_all | solution.py:52
  100.6 181.4 %all-to-all-start.3 = ((f32[2,64,4,1024]{3,2,0,1:T(4,128)}), f32[2,64,4,1024]{3,2,0,1:T(4,128)S(1)}, u32[]{:S(2)}, u32[]{:S(2)}) async-start(f32[2,64,4,1024]{3,2,0,1:T(4,128)} %copy.46), calls=%async_computation.3 | async-start | bytes 4194304 | tf_op jit(solution)/shard_map/all_to_all | solution.py:52
  106.1 519.6 %all-gather.3.cloned.1.call-start = ((), (), s32[]{:S(2)}) async-start(), calls=%async_computation.6 | async-start | bytes 4456448 | tf_op jit(solution)/shard_map/all_gather | solution.py:149
  290.0 1.3 copy-start.2
  290.0 1.3 copy-start.3
  526.8 1.1 copy-start.4
  526.8 1.1 copy-start.5
  526.8 1.1 copy-start.6
  526.8 1.1 copy-start.7
  625.7 3.4 copy-start.1
Sparse Core Ops, SparseCore 0:
  528.0 97.6 all-gather.2
